TPU v7x, 256 devices: a whole 4x4x8 slice. The times are simulated.
256 devices in a mesh: rows: 16 (over y, x), keys: 16 (over z, core).
Axes of the slice: x: 4, y: 4, z: 8, core: 2. Of those that a mesh axis runs over, the one named last changes fastest.
Arguments:
- pair_rep: bfloat16 [768, 768, 128], P('rows', 'keys'), may hold values from -6 to 6
- norm_gain: float32 [128], replicated, may hold values from 0.1 to 1.9
- w_query: bfloat16 [128, 128], replicated, may hold values from -0.5 to 0.5
- w_key: bfloat16 [128, 128], replicated, may hold values from -0.5 to 0.5
- w_value: bfloat16 [128, 128], replicated, may hold values from -0.5 to 0.5
- w_gate: bfloat16 [128, 128], replicated, may hold values from -0.5 to 0.5
- w_out: bfloat16 [128, 128], replicated, may hold values from -0.5 to 0.5
- pair_bias: bfloat16 [4, 768, 768], P(None, 'keys', 'rows'), may hold values from -12 to 300
Outputs:
- update: bfloat16 [768, 768, 128], P('rows', 'keys')
All inputs are finite; a program needn't handle non-finite values.
Results may differ from a plain program's by a relative error of at most 0.025.
Values may be sent and summed in bfloat16 or wider, within the bound.
A program may use at most 128 MiB of HBM per device.

v0:
```python
import jax
import jax.numpy as jnp
from jax import lax
from jax.sharding import Mesh
from jax.sharding import PartitionSpec as P

ROWS = ("rows_0", "rows_1")
epsilon = 1e-05
block_rows = 8


def gathered_by_axis(array, axes, dim):
    out = array
    for number in range(len(axes) - 1, -1, -1):
        out = lax.all_gather(out, axes[number], axis=dim, tiled=True)
    return out


def normalize(pair_rep, norm_gain):
    values = pair_rep.astype(jnp.float32)
    center = jnp.mean(values, axis=-1, keepdims=True)
    spread = jnp.mean(jnp.square(values - center), axis=-1, keepdims=True)
    return ((values - center) * lax.rsqrt(spread + epsilon) * norm_gain).astype(jnp.bfloat16)


def split_heads(tensor, head_count):
    return tensor.reshape(tensor.shape[:-1] + (head_count, tensor.shape[-1] // head_count))


def blocked(tensor):
    return tensor.reshape((tensor.shape[0] // block_rows, block_rows) + tensor.shape[1:])


def unblocked(tensor):
    return tensor.reshape((tensor.shape[0] * tensor.shape[1],) + tensor.shape[2:])


def absorb(running, query_block, key_block, value_block, bias_piece, head_count):
    highest, totals, summed = running
    logits = (
        jnp.einsum(
            "rjhd,rkhd->rhjk",
            split_heads(query_block, head_count),
            split_heads(key_block, head_count),
            preferred_element_type=jnp.float32,
        )
        + bias_piece.astype(jnp.float32)[None]
    )
    new_highest = jnp.maximum(highest, jnp.max(logits, axis=3))
    shrink = jnp.exp(highest - new_highest)
    powers = jnp.exp(logits - new_highest[..., None])
    totals = totals * shrink + jnp.sum(powers, axis=3)
    summed = summed * jnp.transpose(shrink, (0, 2, 1))[..., None] + jnp.einsum(
        "rhjk,rkhd->rjhd",
        powers.astype(jnp.bfloat16),
        split_heads(value_block, head_count),
        preferred_element_type=jnp.float32,
    )
    return (new_highest, totals, summed)


def body(pair_rep, norm_gain, w_query, w_key, w_value, w_gate, w_out, pair_bias):
    head_count = pair_bias.shape[0]
    inner_width = w_query.shape[1]
    normed = normalize(pair_rep, norm_gain)
    local_rows, local_keys = (normed.shape[0], normed.shape[1])
    queries = (
        jnp.dot(normed, w_query, preferred_element_type=jnp.float32)
        * (inner_width // head_count) ** (-0.5)
    ).astype(jnp.bfloat16)
    gates = jax.nn.sigmoid(jnp.dot(normed, w_gate, preferred_element_type=jnp.float32))
    bias_full = gathered_by_axis(pair_bias, ROWS, 2)
    initial = (
        jnp.full((local_rows, head_count, local_keys), -1e30, jnp.float32),
        jnp.zeros((local_rows, head_count, local_keys), jnp.float32),
        jnp.zeros((local_rows, local_keys, head_count, inner_width // head_count), jnp.float32),
    )
    piece = lax.all_gather(normed, "keys", axis=1, tiled=True)

    def one_block(arrays):
        highest, totals, summed, query_block, input_block = arrays
        key_block = jnp.dot(input_block, w_key, preferred_element_type=jnp.float32).astype(
            jnp.bfloat16
        )
        value_block = jnp.dot(input_block, w_value, preferred_element_type=jnp.float32).astype(
            jnp.bfloat16
        )
        return absorb(
            (highest, totals, summed), query_block, key_block, value_block, bias_full, head_count
        )

    results = lax.map(one_block, tuple((blocked(tensor) for tensor in initial + (queries, piece))))
    highest, totals, summed = tuple((unblocked(tensor) for tensor in results))
    attended = summed / jnp.transpose(totals, (0, 2, 1))[..., None]
    attended = attended.reshape(local_rows, local_keys, inner_width)
    gated = (gates * attended).astype(jnp.bfloat16)
    return jnp.dot(gated, w_out, preferred_element_type=jnp.float32).astype(jnp.bfloat16)


def solution(mesh):
    torus = Mesh(mesh.devices.reshape(4, 4, mesh.shape["keys"]), ("rows_0", "rows_1", "keys"))
    placed = (P(ROWS, "keys", None), P(), P(), P(), P(), P(), P(), P(None, "keys", ROWS))
    return jax.shard_map(
        body, mesh=torus, in_specs=placed, out_specs=P(ROWS, "keys", None), check_vma=False
    )
```

profile of v0, /device:TPU:1, one launch (start us, length us, event | category | flops | bytes accessed | tf_op | source)
XLA Modules:
  0.0 142.0 jit_solution(230207090936119171)
XLA Ops:
  6.6 1.5 %convert_reduce_fusion = f32[48,48]{1,0:T(8,128)S(1)} fusion(bf16[48,48,128]{2,1,0:T(8,128)(2,1)} %param.10), kind=kLoop, calls=%fused_computation.27 | loop fusion | flops 587520 | bytes 599040 | tf_op jit(solution)/shard_map/reduce_sum | solution.py:21
  8.1 1.8 %fusion.35 = f32[48,48]{1,0:T(8,128)S(1)} fusion(bf16[48,48,128]{2,1,0:T(8,128)(2,1)} %param.10, f32[48,48]{1,0:T(8,128)S(1)} %broadcast_multiply_fusion), kind=kLoop, calls=%fused_computation.39 | loop fusion | flops 1177344 | bytes 608256 | tf_op jit(solution)/shard_map/reduce_sum | solution.py:22
  9.9 2.2 %fusion.37 = bf16[48,48,128]{2,1,0:T(8,128)(2,1)} fusion(bf16[48,48,128]{2,1,0:T(8,128)(2,1)S(1)} %copy-done.1, f32[128]{0:T(128)} %param.11, f32[48,48]{1,0:T(8,128)S(1)} %add_rsqrt_fusion, f32[48,48]{1,0:T(8,128)S(1)} %broadcast_multiply_fusion), kind=kLoop, calls=%fused_computation.41 | loop fusion | flops 1474560 | bytes 1198592 | tf_op jit(solution)/shard_map/convert_element_type | solution.py:23
  12.4 10.5 %all_gather.10 = bf16[4,48,192]{1,0,2:T(4,128)(2,1)S(1)} all-gather(bf16[4,48,48]{1,0,2:T(4,128)(2,1)S(1)} %copy.25), channel_id=1, replica_groups=mesh['rows_0'=4,'rows_1'=4,'keys'=16] {'rows_1'}, dimensions={2}, use_global_device_ids=true | all-gather | bytes 92160 | tf_op jit(solution)/shard_map/all_gather | solution.py:15
  22.8 12.1 %all_gather.11 = bf16[4,48,768]{1,0,2:T(4,128)(2,1)S(1)} all-gather(bf16[4,48,192]{1,0,2:T(4,128)(2,1)S(1)} %all_gather.10), channel_id=1, replica_groups=mesh['rows_0'=4,'rows_1'=4,'keys'=16] {'rows_0'}, dimensions={2}, use_global_device_ids=true | all-gather | bytes 368640 | tf_op jit(solution)/shard_map/all_gather | solution.py:15
  35.0 0.5 copy.28
  35.6 0.3 fusion.34
  35.9 41.3 %all-gather.2.cloned.1.call-done = bf16[48,768,128]{2,1,0:T(8,128)(2,1)} async-done(((bf16[48,48,128]{2,1,0:T(8,128)(2,1)}), bf16[48,768,128]{2,1,0:T(8,128)(2,1)}) %all-gather.2.cloned.1.call-update) | async-done | bytes 9437200 | tf_op jit(solution)/shard_map/all_gather | solution.py:78
  77.2 49.3 %while.12 = (s32[]{:T(128)}, f32[6,8,4,48]{3,2,1,0:T(4,128)S(1)}, f32[6,8,48,4,32]{2,4,3,1,0:T(8,128)}, bf16[6,8,48,128]{3,2,1,0:T(8,128)(2,1)S(1)}, bf16[6,8,76...) while((s32[]{:T(128)}, f32[6,8,4,48]{3,2,1,0:T(4,128)S(1)}, ...), condition=%wide.region_5.6_spmd, body=%wide.region_2.5_spmd.sunk | while | flops 564862464 | bytes 27426936 | solution.py:92
  77.3 0.2 copy.34
  77.5 2.0 %convolution_convert_fusion.5 = bf16[8,768,128]{1,2,0:T(8,128)(2,1)S(1)} fusion(bf16[6,8,768,128]{3,2,1,0:T(8,128)(2,1)} %get-tuple-element.181, s32[]{:T(128)S(6)} %copy.40, bf16[128,128]{0,1:T(8,128)(2,1)S(1)} %get-tuple-element.182), kind=kOutput, calls=%fused_computation.8.clone.1 | convolution fusion | flops 202113024 | bytes 3178500 | tf_op jit(solution)/shard_map/while/body/eval_jaxpr/dot_general | solution.py:82
  79.5 1.0 add_reduce_fusion.2
  80.5 1.1 fusion.70
  81.6 2.0 %convolution_convert_fusion.6 = bf16[8,768,128]{1,2,0:T(8,128)(2,1)S(1)} fusion(bf16[6,8,768,128]{3,2,1,0:T(8,128)(2,1)} %get-tuple-element.181, s32[]{:T(128)S(6)} %copy.40, bf16[128,128]{0,1:T(8,128)(2,1)S(1)} %get-tuple-element.184), kind=kOutput, calls=%fused_computation.7.clone.1 | convolution fusion | flops 202113024 | bytes 3178500 | tf_op jit(solution)/shard_map/while/body/eval_jaxpr/dot_general | solution.py:85
  83.6 1.9 %fusion.71 = f32[6,8,48,4,32]{2,4,3,1,0:T(8,128)} fusion(f32[6,8,48,4,32]{2,4,3,1,0:T(8,128)} %get-tuple-element.170, s32[]{:T(128)S(6)} %copy.40, bf16[8,768,4,32]{1,3,2,0:T(8,128)(2,1)S(1)} %bitcast.81, f32[8,4,48,768]{3,2,1,0:T(8,128)S(1)} %get-tuple-element.155, f32[8,4,48]{2,1,0:T(4,128)S(1)} %get-tuple-element.157, ...), kind=kOutput, calls=%fused_computation.16.clone.1 | convolution fusion | flops 79085568 | bytes 7417860 | tf_op jit(solution)/shard_map/while/body/eval_jaxpr/rhjk,rkhd->rjhd/dot_general | solution.py:53
  85.5 0.2 copy.34
  85.7 2.0 %convolution_convert_fusion.5 = bf16[8,768,128]{1,2,0:T(8,128)(2,1)S(1)} fusion(bf16[6,8,768,128]{3,2,1,0:T(8,128)(2,1)} %get-tuple-element.181, s32[]{:T(128)S(6)} %copy.40, bf16[128,128]{0,1:T(8,128)(2,1)S(1)} %get-tuple-element.182), kind=kOutput, calls=%fused_computation.8.clone.1 | convolution fusion | flops 202113024 | bytes 3178500 | tf_op jit(solution)/shard_map/while/body/eval_jaxpr/dot_general | solution.py:82
  87.7 1.0 add_reduce_fusion.2
  88.7 1.1 fusion.70
  89.8 2.0 %convolution_convert_fusion.6 = bf16[8,768,128]{1,2,0:T(8,128)(2,1)S(1)} fusion(bf16[6,8,768,128]{3,2,1,0:T(8,128)(2,1)} %get-tuple-element.181, s32[]{:T(128)S(6)} %copy.40, bf16[128,128]{0,1:T(8,128)(2,1)S(1)} %get-tuple-element.184), kind=kOutput, calls=%fused_computation.7.clone.1 | convolution fusion | flops 202113024 | bytes 3178500 | tf_op jit(solution)/shard_map/while/body/eval_jaxpr/dot_general | solution.py:85
  91.8 1.9 %fusion.71 = f32[6,8,48,4,32]{2,4,3,1,0:T(8,128)} fusion(f32[6,8,48,4,32]{2,4,3,1,0:T(8,128)} %get-tuple-element.170, s32[]{:T(128)S(6)} %copy.40, bf16[8,768,4,32]{1,3,2,0:T(8,128)(2,1)S(1)} %bitcast.81, f32[8,4,48,768]{3,2,1,0:T(8,128)S(1)} %get-tuple-element.155, f32[8,4,48]{2,1,0:T(4,128)S(1)} %get-tuple-element.157, ...), kind=kOutput, calls=%fused_computation.16.clone.1 | convolution fusion | flops 79085568 | bytes 7417860 | tf_op jit(solution)/shard_map/while/body/eval_jaxpr/rhjk,rkhd->rjhd/dot_general | solution.py:53
  93.7 0.2 copy.34
  93.9 2.0 %convolution_convert_fusion.5 = bf16[8,768,128]{1,2,0:T(8,128)(2,1)S(1)} fusion(bf16[6,8,768,128]{3,2,1,0:T(8,128)(2,1)} %get-tuple-element.181, s32[]{:T(128)S(6)} %copy.40, bf16[128,128]{0,1:T(8,128)(2,1)S(1)} %get-tuple-element.182), kind=kOutput, calls=%fused_computation.8.clone.1 | convolution fusion | flops 202113024 | bytes 3178500 | tf_op jit(solution)/shard_map/while/body/eval_jaxpr/dot_general | solution.py:82
  95.9 1.0 add_reduce_fusion.2
  96.9 1.1 fusion.70
  98.0 2.0 %convolution_convert_fusion.6 = bf16[8,768,128]{1,2,0:T(8,128)(2,1)S(1)} fusion(bf16[6,8,768,128]{3,2,1,0:T(8,128)(2,1)} %get-tuple-element.181, s32[]{:T(128)S(6)} %copy.40, bf16[128,128]{0,1:T(8,128)(2,1)S(1)} %get-tuple-element.184), kind=kOutput, calls=%fused_computation.7.clone.1 | convolution fusion | flops 202113024 | bytes 3178500 | tf_op jit(solution)/shard_map/while/body/eval_jaxpr/dot_general | solution.py:85
  100.0 1.9 %fusion.71 = f32[6,8,48,4,32]{2,4,3,1,0:T(8,128)} fusion(f32[6,8,48,4,32]{2,4,3,1,0:T(8,128)} %get-tuple-element.170, s32[]{:T(128)S(6)} %copy.40, bf16[8,768,4,32]{1,3,2,0:T(8,128)(2,1)S(1)} %bitcast.81, f32[8,4,48,768]{3,2,1,0:T(8,128)S(1)} %get-tuple-element.155, f32[8,4,48]{2,1,0:T(4,128)S(1)} %get-tuple-element.157, ...), kind=kOutput, calls=%fused_computation.16.clone.1 | convolution fusion | flops 79085568 | bytes 7417860 | tf_op jit(solution)/shard_map/while/body/eval_jaxpr/rhjk,rkhd->rjhd/dot_general | solution.py:53
  102.0 0.2 copy.34
  102.1 2.0 %convolution_convert_fusion.5 = bf16[8,768,128]{1,2,0:T(8,128)(2,1)S(1)} fusion(bf16[6,8,768,128]{3,2,1,0:T(8,128)(2,1)} %get-tuple-element.181, s32[]{:T(128)S(6)} %copy.40, bf16[128,128]{0,1:T(8,128)(2,1)S(1)} %get-tuple-element.182), kind=kOutput, calls=%fused_computation.8.clone.1 | convolution fusion | flops 202113024 | bytes 3178500 | tf_op jit(solution)/shard_map/while/body/eval_jaxpr/dot_general | solution.py:82
  104.1 1.0 add_reduce_fusion.2
  105.2 1.1 fusion.70
  106.2 2.0 %convolution_convert_fusion.6 = bf16[8,768,128]{1,2,0:T(8,128)(2,1)S(1)} fusion(bf16[6,8,768,128]{3,2,1,0:T(8,128)(2,1)} %get-tuple-element.181, s32[]{:T(128)S(6)} %copy.40, bf16[128,128]{0,1:T(8,128)(2,1)S(1)} %get-tuple-element.184), kind=kOutput, calls=%fused_computation.7.clone.1 | convolution fusion | flops 202113024 | bytes 3178500 | tf_op jit(solution)/shard_map/while/body/eval_jaxpr/dot_general | solution.py:85
  108.2 1.9 %fusion.71 = f32[6,8,48,4,32]{2,4,3,1,0:T(8,128)} fusion(f32[6,8,48,4,32]{2,4,3,1,0:T(8,128)} %get-tuple-element.170, s32[]{:T(128)S(6)} %copy.40, bf16[8,768,4,32]{1,3,2,0:T(8,128)(2,1)S(1)} %bitcast.81, f32[8,4,48,768]{3,2,1,0:T(8,128)S(1)} %get-tuple-element.155, f32[8,4,48]{2,1,0:T(4,128)S(1)} %get-tuple-element.157, ...), kind=kOutput, calls=%fused_computation.16.clone.1 | convolution fusion | flops 79085568 | bytes 7417860 | tf_op jit(solution)/shard_map/while/body/eval_jaxpr/rhjk,rkhd->rjhd/dot_general | solution.py:53
  110.2 0.2 copy.34
  110.4 2.0 %convolution_convert_fusion.5 = bf16[8,768,128]{1,2,0:T(8,128)(2,1)S(1)} fusion(bf16[6,8,768,128]{3,2,1,0:T(8,128)(2,1)} %get-tuple-element.181, s32[]{:T(128)S(6)} %copy.40, bf16[128,128]{0,1:T(8,128)(2,1)S(1)} %get-tuple-element.182), kind=kOutput, calls=%fused_computation.8.clone.1 | convolution fusion | flops 202113024 | bytes 3178500 | tf_op jit(solution)/shard_map/while/body/eval_jaxpr/dot_general | solution.py:82
  112.4 1.0 add_reduce_fusion.2
  113.4 1.1 fusion.70
  114.5 2.0 %convolution_convert_fusion.6 = bf16[8,768,128]{1,2,0:T(8,128)(2,1)S(1)} fusion(bf16[6,8,768,128]{3,2,1,0:T(8,128)(2,1)} %get-tuple-element.181, s32[]{:T(128)S(6)} %copy.40, bf16[128,128]{0,1:T(8,128)(2,1)S(1)} %get-tuple-element.184), kind=kOutput, calls=%fused_computation.7.clone.1 | convolution fusion | flops 202113024 | bytes 3178500 | tf_op jit(solution)/shard_map/while/body/eval_jaxpr/dot_general | solution.py:85
  116.5 1.9 %fusion.71 = f32[6,8,48,4,32]{2,4,3,1,0:T(8,128)} fusion(f32[6,8,48,4,32]{2,4,3,1,0:T(8,128)} %get-tuple-element.170, s32[]{:T(128)S(6)} %copy.40, bf16[8,768,4,32]{1,3,2,0:T(8,128)(2,1)S(1)} %bitcast.81, f32[8,4,48,768]{3,2,1,0:T(8,128)S(1)} %get-tuple-element.155, f32[8,4,48]{2,1,0:T(4,128)S(1)} %get-tuple-element.157, ...), kind=kOutput, calls=%fused_computation.16.clone.1 | convolution fusion | flops 79085568 | bytes 7417860 | tf_op jit(solution)/shard_map/while/body/eval_jaxpr/rhjk,rkhd->rjhd/dot_general | solution.py:53
  118.6 2.0 %convolution_convert_fusion.5 = bf16[8,768,128]{1,2,0:T(8,128)(2,1)S(1)} fusion(bf16[6,8,768,128]{3,2,1,0:T(8,128)(2,1)} %get-tuple-element.181, s32[]{:T(128)S(6)} %copy.40, bf16[128,128]{0,1:T(8,128)(2,1)S(1)} %get-tuple-element.182), kind=kOutput, calls=%fused_computation.8.clone.1 | convolution fusion | flops 202113024 | bytes 3178500 | tf_op jit(solution)/shard_map/while/body/eval_jaxpr/dot_general | solution.py:82
  120.6 1.0 add_reduce_fusion.2
  121.6 1.1 fusion.70
  122.7 2.0 %convolution_convert_fusion.6 = bf16[8,768,128]{1,2,0:T(8,128)(2,1)S(1)} fusion(bf16[6,8,768,128]{3,2,1,0:T(8,128)(2,1)} %get-tuple-element.181, s32[]{:T(128)S(6)} %copy.40, bf16[128,128]{0,1:T(8,128)(2,1)S(1)} %get-tuple-element.184), kind=kOutput, calls=%fused_computation.7.clone.1 | convolution fusion | flops 202113024 | bytes 3178500 | tf_op jit(solution)/shard_map/while/body/eval_jaxpr/dot_general | solution.py:85
  124.7 1.9 %fusion.71 = f32[6,8,48,4,32]{2,4,3,1,0:T(8,128)} fusion(f32[6,8,48,4,32]{2,4,3,1,0:T(8,128)} %get-tuple-element.170, s32[]{:T(128)S(6)} %copy.40, bf16[8,768,4,32]{1,3,2,0:T(8,128)(2,1)S(1)} %bitcast.81, f32[8,4,48,768]{3,2,1,0:T(8,128)S(1)} %get-tuple-element.155, f32[8,4,48]{2,1,0:T(4,128)S(1)} %get-tuple-element.157, ...), kind=kOutput, calls=%fused_computation.16.clone.1 | convolution fusion | flops 79085568 | bytes 7417860 | tf_op jit(solution)/shard_map/while/body/eval_jaxpr/rhjk,rkhd->rjhd/dot_general | solution.py:53
  126.5 3.1 %copy.30 = f32[48,48,128]{2,1,0:T(8,128)} copy(f32[48,48,128]{1,2,0:T(8,128)} %bitcast.85) | data formatting | bytes 2359296 | tf_op jit(solution)/shard_map/reshape | solution.py:35
  129.7 0.2 div.23
  129.9 2.0 %copy.31 = f32[48,48,128]{2,1,0:T(8,128)} copy(f32[48,48,128]{1,2,0:T(8,128)S(1)} %bitcast.84) | data formatting | bytes 2359296 | tf_op jit(solution)/shard_map/div | solution.py:94
  131.9 3.3 %convolution_convert_fusion.2 = bf16[48,48,128]{2,1,0:T(8,128)(2,1)} fusion(bf16[48,48,128]{2,1,0:T(8,128)(2,1)} %fusion.37, f32[48,48,128]{2,1,0:T(8,128)} %copy.30, f32[48,48,128]{2,1,0:T(8,128)} %copy.31, bf16[128,128]{1,0:T(8,128)(2,1)S(1)} %copy-done.6, bf16[128,128]{1,0:T(8,128)(2,1)S(1)} %copy-done.7), kind=kOutput, calls=%fused_computation.38 | convolution fusion | flops 153059328 | bytes 3604480 | tf_op jit(solution)/shard_map/dot_general | solution.py:97
  (50 shorter events, 1.3 us)
Async XLA Ops:
  6.5 29.1 %copy-start = (bf16[128,128]{1,0:T(8,128)(2,1)S(1)}, bf16[128,128]{1,0:T(8,128)(2,1)}, u32[]{:S(2)}) copy-start(bf16[128,128]{1,0:T(8,128)(2,1)} %param.12) | copy-start | bytes 98308
  6.5 3.3 %copy-start.1 = (bf16[48,48,128]{2,1,0:T(8,128)(2,1)S(1)}, bf16[48,48,128]{2,1,0:T(8,128)(2,1)}, u32[]{:S(2)}) copy-start(bf16[48,48,128]{2,1,0:T(8,128)(2,1)} %param.10) | copy-start | bytes 1769476
  6.5 5.6 %copy-start.4 = (bf16[128,128]{1,0:T(8,128)(2,1)S(1)}, bf16[128,128]{1,0:T(8,128)(2,1)}, u32[]{:S(2)}) copy-start(bf16[128,128]{1,0:T(8,128)(2,1)} %param.13) | copy-start | bytes 98308
  6.5 5.7 %copy-start.3 = (bf16[4,48,48]{2,1,0:T(8,128)(2,1)S(1)}, bf16[4,48,48]{2,1,0:T(8,128)(2,1)}, u32[]{:S(2)}) copy-start(bf16[4,48,48]{2,1,0:T(8,128)(2,1)} %param.17) | copy-start | bytes 55300
  6.5 70.7 %all-gather.2.cloned.1.call-start = ((), (), s32[]{:S(2)}) async-start(), calls=%async_computation | async-start | bytes 10027008 | tf_op jit(solution)/shard_map/all_gather | solution.py:78
  12.1 23.4 %copy-start.5 = (bf16[128,128]{1,0:T(8,128)(2,1)S(1)}, bf16[128,128]{1,0:T(8,128)(2,1)}, u32[]{:S(2)}) copy-start(bf16[128,128]{1,0:T(8,128)(2,1)} %param.14) | copy-start | bytes 98308
  12.1 23.5 %copy-start.2 = (bf16[48,48,128]{2,1,0:T(8,128)(2,1)S(1)}, bf16[48,48,128]{2,1,0:T(8,128)(2,1)}, u32[]{:S(2)}) copy-start(bf16[48,48,128]{2,1,0:T(8,128)(2,1)} %fusion.37) | copy-start | bytes 1769476
  129.9 2.0 %copy-start.6 = (bf16[128,128]{1,0:T(8,128)(2,1)S(1)}, bf16[128,128]{1,0:T(8,128)(2,1)}, u32[]{:S(2)}) copy-start(bf16[128,128]{1,0:T(8,128)(2,1)} %param.16) | copy-start | bytes 98308
  129.9 2.0 %copy-start.7 = (bf16[128,128]{1,0:T(8,128)(2,1)S(1)}, bf16[128,128]{1,0:T(8,128)(2,1)}, u32[]{:S(2)}) copy-start(bf16[128,128]{1,0:T(8,128)(2,1)} %param.15) | copy-start | bytes 98308
Sparse Core Ops, SparseCore 0:
  12.2 64.9 all-gather.1
where the time goes:
time: 143 us; the launch traced here: 142 us
  matrix products  44.6 us (31%)
  waiting for transfers between devices  41.3 us (29%)
  blocking collectives  22.6 us (16%)
  between operations  13.5 us (9%)
  other arithmetic  12.3 us (9%)
  local copies, waits for them, and re-layouts  7.34 us (5%)
    all_gather x1, waiting for transfers between devices, body(): piece = lax.all_gather(normed, 'keys', axis=1, tiled=True)  41.3 us
    all_gather x2, blocking collectives, gathered_by_axis(): out = lax.all_gather(out, axes[number], axis=dim, tiled=True)  22.6 us
    dot_general x6, matrix products, one_block(): jnp.dot(input_block, w_value, preferred_element_type=jnp.float32)  11.9 us
    dot_general x6, matrix products, one_block(): jnp.dot(input_block, w_key, preferred_element_type=jnp.float32)  11.9 us
    dot_general x6, matrix products, absorb(): jnp.einsum('rhjk,rkhd->rjhd', powers.astype(jnp.bfloat16), split_heads(va...  11.2 us
    reduce_sum x6, other arithmetic, absorb(): totals = totals * shrink + jnp.sum(powers, axis=3)  6.3 us
    dot_general x6, matrix products, absorb(): jnp.einsum('rjhd,rkhd->rhjk', split_heads(query_block, head_count), split...  5.99 us
    dot_general x1, matrix products, body(): jnp.dot(gated, w_out, preferred_element_type=jnp.float32)  3.32 us
  transfers between devices with their start and end apart: 1, of which 1 were waited for; matrix products, arithmetic and copies ran while one was open for 1% of the time, Pallas kernels for 0%

commit v1 on v0

--- a/solution.py
+++ b/solution.py
@@ -75,7 +75,9 @@
         jnp.zeros((local_rows, head_count, local_keys), jnp.float32),
         jnp.zeros((local_rows, local_keys, head_count, inner_width // head_count), jnp.float32),
     )
-    piece = lax.all_gather(normed, "keys", axis=1, tiled=True)
+    piece = jnp.concatenate(
+        lax.all_to_all(jnp.stack([normed] * lax.axis_size("keys")), "keys", 0, 0), axis=1
+    )
 
     def one_block(arrays):
         highest, totals, summed, query_block, input_block = arrays

time: 143 us -> 295 us (2.06)
  waiting for transfers between devices: 41.3 us -> 182 us
  local copies, waits for them, and re-layouts: 7.34 us -> 22.8 us
  between operations: 13.5 us -> 0.17 us
  starting transfers between devices: 0.03 us -> 10.1 us
    all_to_all x0 -> x1, waiting for transfers between devices: none -> 182 us  [body(): lax.all_to_all(jnp.stack([normed] * lax.axis_size('keys')), 'keys', 0, 0)]
    all_gather x1 -> x0, waiting for transfers between devices: 41.3 us -> none  [body(): piece = lax.all_gather(normed, 'keys', axis=1, tiled=True)]
    all_to_all x0 -> x1, starting transfers between devices: none -> 10.1 us  [body(): lax.all_to_all(jnp.stack([normed] * lax.axis_size('keys')), 'keys', 0, 0)]
    all_to_all x0 -> x1, local copies, waits for them, and re-layouts: none -> 10 us  [body(): lax.all_to_all(jnp.stack([normed] * lax.axis_size('keys')), 'keys', 0, 0)]
    another operation x0 -> x1, local copies, waits for them, and re-layouts: none -> 5.44 us  [body(): jnp.stack([normed] * lax.axis_size('keys'))]
  transfers between devices with their start and end apart: 1 -> 1, of which waited for: 1 -> 1; matrix products, arithmetic and copies ran while one was open for 1% -> 0% of each run, Pallas kernels for 0% -> 0%
where the time goes in v1:
time: 295 us; the launch traced here: 294 us
  waiting for transfers between devices  182 us (62%)
  matrix products  44.6 us (15%)
  blocking collectives  23.1 us (8%)
  local copies, waits for them, and re-layouts  22.8 us (8%)
  other arithmetic  11.6 us (4%)
  starting transfers between devices  10.1 us (3%)
    all_to_all x1, waiting for transfers between devices, body(): lax.all_to_all(jnp.stack([normed] * lax.axis_size('keys')), 'keys', 0, 0)  182 us
    all_gather x2, blocking collectives, gathered_by_axis(): out = lax.all_gather(out, axes[number], axis=dim, tiled=True)  23.1 us
    dot_general x6, matrix products, one_block(): jnp.dot(input_block, w_value, preferred_element_type=jnp.float32)  11.9 us
    dot_general x6, matrix products, one_block(): jnp.dot(input_block, w_key, preferred_element_type=jnp.float32)  11.9 us
    dot_general x6, matrix products, absorb(): jnp.einsum('rhjk,rkhd->rjhd', powers.astype(jnp.bfloat16), split_heads(va...  11.2 us
    all_to_all x1, starting transfers between devices, body(): lax.all_to_all(jnp.stack([normed] * lax.axis_size('keys')), 'keys', 0, 0)  10.1 us
    all_to_all x1, local copies, waits for them, and re-layouts, body(): lax.all_to_all(jnp.stack([normed] * lax.axis_size('keys')), 'keys', 0, 0)  10 us
    reduce_sum x6, other arithmetic, absorb(): totals = totals * shrink + jnp.sum(powers, axis=3)  6.3 us
  transfers between devices with their start and end apart: 1, of which 1 were waited for; matrix products, arithmetic and copies ran while one was open for 0% of the time, Pallas kernels for 0%

profile of v1, /device:TPU:1, one launch (start us, length us, event | category | flops | bytes accessed | tf_op | source)
XLA Modules:
  0.0 294.2 jit_solution(1822956246215462606)
XLA Ops:
  0.0 1.5 convert_reduce_fusion
  1.5 1.8 fusion.35
  3.3 1.4 fusion.37
  4.8 5.4 %stack.2 = bf16[16,48,48,128]{3,2,1,0:T(8,128)(2,1)} broadcast(bf16[48,48,128]{2,1,0:T(8,128)(2,1)S(1)} %fusion.37), dimensions={1,2,3} | broadcast | bytes 10027008 | tf_op jit(solution)/shard_map/stack | solution.py:79
  10.2 10.1 %all-to-all-start = ((bf16[16,48,48,128]{3,2,1,0:T(8,128)(2,1)}), bf16[16,48,48,128]{3,2,1,0:T(8,128)(2,1)}, u32[]{:S(2)}, u32[]{:S(2)}) async-start(bf16[16,48,48,128]{3,2,1,0:T(8,128)(2,1)} %stack.2), calls=%async_computation | async-start | bytes 18874368 | tf_op jit(solution)/shard_map/all_to_all | solution.py:79
  20.6 10.4 %all_gather.6 = bf16[4,48,192]{1,0,2:T(4,128)(2,1)S(1)} all-gather(bf16[4,48,48]{1,0,2:T(4,128)(2,1)S(1)} %copy.26), channel_id=1, replica_groups=mesh['rows_0'=4,'rows_1'=4,'keys'=16] {'rows_1'}, dimensions={2}, use_global_device_ids=true | all-gather | bytes 92160 | tf_op jit(solution)/shard_map/all_gather | solution.py:15
  31.0 12.7 %all_gather.7 = bf16[4,48,768]{1,0,2:T(4,128)(2,1)S(1)} all-gather(bf16[4,48,192]{1,0,2:T(4,128)(2,1)S(1)} %all_gather.6), channel_id=1, replica_groups=mesh['rows_0'=4,'rows_1'=4,'keys'=16] {'rows_0'}, dimensions={2}, use_global_device_ids=true | all-gather | bytes 368640 | tf_op jit(solution)/shard_map/all_gather | solution.py:15
  43.7 0.5 copy.29
  44.3 0.3 fusion.34
  44.6 181.5 %all-to-all-done = bf16[16,48,48,128]{3,2,1,0:T(8,128)(2,1)} async-done(((bf16[16,48,48,128]{3,2,1,0:T(8,128)(2,1)}), bf16[16,48,48,128]{3,2,1,0:T(8,128)(2,1)}, u32[]{:S(2)}, u32[]{:S(2)}) %all-to-all-start) | async-done | bytes 9437216 | tf_op jit(solution)/shard_map/all_to_all | solution.py:79
  226.2 10.0 %copy.25 = bf16[16,48,48,128]{3,2,0,1:T(8,128)(2,1)} copy(bf16[16,48,48,128]{3,2,1,0:T(8,128)(2,1)} %all-to-all-done) | data formatting | bytes 18874368 | tf_op jit(solution)/shard_map/all_to_all | solution.py:79
  236.2 49.3 %while.12 = (s32[]{:T(128)}, f32[6,8,4,48]{3,2,1,0:T(4,128)S(1)}, f32[6,8,48,4,32]{2,4,3,1,0:T(8,128)}, bf16[6,8,48,128]{3,2,1,0:T(8,128)(2,1)S(1)}, bf16[6,8,76...) while((s32[]{:T(128)}, f32[6,8,4,48]{3,2,1,0:T(4,128)S(1)}, ...), condition=%wide.region_5.6_spmd, body=%wide.region_2.5_spmd.sunk | while | flops 564862464 | bytes 27426936 | solution.py:94
  236.3 0.2 copy.35
  236.4 2.0 convolution_convert_fusion.5
  238.4 1.0 add_reduce_fusion.2
  239.5 1.1 fusion.70
  240.5 2.0 convolution_convert_fusion.6
  242.5 1.9 fusion.71
  244.6 2.0 convolution_convert_fusion.5
  246.6 1.0 add_reduce_fusion.2
  247.7 1.1 fusion.70
  248.8 2.0 convolution_convert_fusion.6
  250.7 1.9 fusion.71
  252.9 2.0 convolution_convert_fusion.5
  254.9 1.0 add_reduce_fusion.2
  255.9 1.1 fusion.70
  257.0 2.0 convolution_convert_fusion.6
  259.0 1.9 fusion.71
  260.9 0.2 copy.35
  261.1 2.0 convolution_convert_fusion.5
  263.1 1.0 add_reduce_fusion.2
  264.1 1.1 fusion.70
  265.2 2.0 convolution_convert_fusion.6
  267.2 1.9 fusion.71
  269.3 2.0 convolution_convert_fusion.5
  271.3 1.0 add_reduce_fusion.2
  272.3 1.1 fusion.70
  273.4 2.0 convolution_convert_fusion.6
  275.4 1.9 fusion.71
  277.5 2.0 convolution_convert_fusion.5
  279.5 1.0 add_reduce_fusion.2
  280.5 1.1 fusion.70
  281.6 2.0 convolution_convert_fusion.6
  283.6 1.9 fusion.71
  285.5 3.1 %copy.31 = f32[48,48,128]{2,1,0:T(8,128)} copy(f32[48,48,128]{1,2,0:T(8,128)} %bitcast.87) | data formatting | bytes 2359296 | tf_op jit(solution)/shard_map/reshape | solution.py:35
  288.6 0.2 div.23
  288.9 2.0 copy.32
  290.9 3.3 %convolution_convert_fusion.2 = bf16[48,48,128]{2,1,0:T(8,128)(2,1)} fusion(bf16[48,48,128]{2,1,0:T(8,128)(2,1)} %copy-done.1, f32[48,48,128]{2,1,0:T(8,128)} %copy.31, f32[48,48,128]{2,1,0:T(8,128)} %copy.32, bf16[128,128]{1,0:T(8,128)(2,1)S(1)} %copy-done.6, bf16[128,128]{1,0:T(8,128)(2,1)S(1)} %copy-done.7), kind=kOutput, calls=%fused_computation.38 | convolution fusion | flops 153059328 | bytes 3604480 | tf_op jit(solution)/shard_map/dot_general | solution.py:99
  (51 shorter events, 1.7 us)
Async XLA Ops:
  0.0 44.3 %copy-start = (bf16[128,128]{1,0:T(8,128)(2,1)S(1)}, bf16[128,128]{1,0:T(8,128)(2,1)}, u32[]{:S(2)}) copy-start(bf16[128,128]{1,0:T(8,128)(2,1)} %param.12) | copy-start | bytes 98308
  0.0 3.3 %copy-start.2 = (bf16[48,48,128]{2,1,0:T(8,128)(2,1)S(1)}, bf16[48,48,128]{2,1,0:T(8,128)(2,1)}, u32[]{:S(2)}) copy-start(bf16[48,48,128]{2,1,0:T(8,128)(2,1)} %param.10) | copy-start | bytes 1769476
  4.8 39.5 %copy-start.1 = (bf16[48,48,128]{2,1,0:T(8,128)(2,1)}, bf16[48,48,128]{2,1,0:T(8,128)(2,1)S(1)}, u32[]{:S(2)}) copy-start(bf16[48,48,128]{2,1,0:T(8,128)(2,1)S(1)} %fusion.37) | copy-start | bytes 1769476
  10.2 10.1 %copy-start.4 = (bf16[128,128]{1,0:T(8,128)(2,1)S(1)}, bf16[128,128]{1,0:T(8,128)(2,1)}, u32[]{:S(2)}) copy-start(bf16[128,128]{1,0:T(8,128)(2,1)} %param.13) | copy-start | bytes 98308
  10.2 10.3 %copy-start.3 = (bf16[4,48,48]{2,1,0:T(8,128)(2,1)S(1)}, bf16[4,48,48]{2,1,0:T(8,128)(2,1)}, u32[]{:S(2)}) copy-start(bf16[4,48,48]{2,1,0:T(8,128)(2,1)} %param.17) | copy-start | bytes 55300
  10.2 215.9 %all-to-all-start = ((bf16[16,48,48,128]{3,2,1,0:T(8,128)(2,1)}), bf16[16,48,48,128]{3,2,1,0:T(8,128)(2,1)}, u32[]{:S(2)}, u32[]{:S(2)}) async-start(bf16[16,48,48,128]{3,2,1,0:T(8,128)(2,1)} %stack.2), calls=%async_computation | async-start | bytes 18874368 | tf_op jit(solution)/shard_map/all_to_all | solution.py:79
  20.3 23.9 %copy-start.5 = (bf16[128,128]{1,0:T(8,128)(2,1)S(1)}, bf16[128,128]{1,0:T(8,128)(2,1)}, u32[]{:S(2)}) copy-start(bf16[128,128]{1,0:T(8,128)(2,1)} %param.14) | copy-start | bytes 98308
  288.9 2.0 copy-start.6
  288.9 2.0 copy-start.7
